TPU v7x, 32 devices: a whole 2x2x4 slice. The times are simulated.
32 devices in a mesh: rows: 8 (over z, x), cols: 4 (over y, core).
Axes of the slice: x: 2, y: 2, z: 4, core: 2. Of those that a mesh axis runs over, the one named last changes fastest.
Arguments:
- source_coords: float32 [3, 128, 128], P(None, ('rows', 'cols')), may hold values from -2 to 5
- target_coords: float32 [3, 128, 128], P(None, ('rows', 'cols')), may hold values from -2 to 5
- source_logmass: float32 [128, 128], P(('rows', 'cols')), may hold values from -4 to 134
- target_logmass: float32 [128, 128], P(('rows', 'cols')), may hold values from -4 to 134
- pair_targets: int32 [128, 8], P(('rows', 'cols')), may hold values from 0 to 127, as said below
- pair_counts: int32 [128], P(('rows', 'cols')), may hold values from 1 to 8
Outputs:
- source_potential: float32 [128, 128], P(('rows', 'cols'))
- target_potential: float32 [128, 128], P(('rows', 'cols'))
Inputs may be any that keep to these rules, and one draw needn't show every extreme that they name: `pair_targets`: slot 0 of source cluster s holds s itself. Every other used slot names a target cluster held by a device of the same cols index and another rows index. Over the used slots 1 and later of all source clusters of one device, at most 4 name target clusters of one device, and on every device some device is named exactly 4 times. Unused slots hold cluster numbers that are ignored.
All inputs are finite; a program needn't handle non-finite values.
Results may differ from a plain program's by a relative error of at most 0.0003.
Values sent between devices are 32-bit elements; how exact they have to be, the bound alone decides.
No kernel may reach another device: no remote copies, remote signals or barrier semaphores. Data moves between devices by JAX's collectives and lax.ppermute only.
A program may use at most 64 MiB of HBM per device.

v0:
```python
import math
import jax
import jax.numpy as jnp
from jax import lax
from jax.sharding import PartitionSpec as P

C_ITERS = 4
F_ITERS = 2
NEGATIVE = -1e30
EPS_C = 0.5
EPS_F = 0.1
RHO = 1.0
TAU_C = RHO / (RHO + EPS_C)
TAU_F = RHO / (RHO + EPS_F)


def joined(part, axis, combine):
    gathered = jax.tree.map(lambda a: lax.all_gather(a, axis), part)

    def take(source):
        return jax.tree.map(lambda a: lax.dynamic_index_in_dim(a, source, 0, False), gathered)

    return lax.fori_loop(
        1, lax.axis_size(axis), lambda source, state: combine(state, take(source)), take(0)
    )


def log_total(values, over_axes):
    highest = jnp.max(values, axis=over_axes, keepdims=True)
    summed = jnp.sum(jnp.exp(values - highest), axis=over_axes)
    return jnp.squeeze(highest, over_axes) + jnp.log(summed)


def coarse_cost(cent_self, cent_other):
    distance = (cent_self[0][:, None] - cent_other[0][None, :]) ** 2
    distance = distance + (cent_self[1][:, None] - cent_other[1][None, :]) ** 2
    distance = distance + (cent_self[2][:, None] - cent_other[2][None, :]) ** 2
    return distance


def coarse_update(pot_other, mass_other, cent_self, cent_other):
    scores = mass_other[None, :] + (pot_other[None, :] - coarse_cost(cent_self, cent_other)) / EPS_C
    return -TAU_C * EPS_C * log_total(scores, 1)


def coarse_blocks(pot_other, mass_other, cent_self, cent_other):
    count = cent_self.shape[1]
    width = math.gcd(count, 8)
    portions = cent_self.reshape(3, count // width, width).transpose(1, 0, 2)
    result = lax.map(
        lambda portion: coarse_update(pot_other, mass_other, portion, cent_other), portions
    )
    return result.reshape(count)


def merge_parts(first, second):
    highest = jnp.maximum(first[0], second[0])
    return (
        highest,
        first[1] * jnp.exp(first[0] - highest) + second[1] * jnp.exp(second[0] - highest),
    )


def column_partials(src_mass, src_pot, src_cent, cent_other):
    count = src_cent.shape[1]
    width = math.gcd(count, 8)
    cent_groups = src_cent.reshape(3, count // width, width).transpose(1, 0, 2)
    mass_groups = src_mass.reshape(count // width, width)
    pot_groups = src_pot.reshape(count // width, width)
    columns = cent_other.shape[1]
    start = (jnp.full((columns,), NEGATIVE, jnp.float32), jnp.zeros((columns,), jnp.float32))

    def step(carry, inputs):
        cent_group, mass_group, pot_group = inputs
        scores = (
            mass_group[:, None] + (pot_group[:, None] - coarse_cost(cent_group, cent_other)) / EPS_C
        )
        highest = jnp.max(scores, axis=0)
        summed = jnp.sum(jnp.exp(scores - highest[None, :]), axis=0)
        return (merge_parts(carry, (highest, summed)), None)

    result, unused = lax.scan(step, start, (cent_groups, mass_groups, pot_groups))
    return result


def pair_cost(src_group, tgt_group):
    distance = (src_group[:, 0, None, :, None] - tgt_group[:, 0, :, None, :]) ** 2
    distance = distance + (src_group[:, 1, None, :, None] - tgt_group[:, 1, :, None, :]) ** 2
    distance = distance + (src_group[:, 2, None, :, None] - tgt_group[:, 2, :, None, :]) ** 2
    return distance


def fine_rows(distance, tgt_mass, tgt_pot, usable):
    scores = tgt_mass[:, :, None, :] + (tgt_pot[:, :, None, :] - distance) / EPS_F
    scores = jnp.where(usable[:, :, None, None], scores, NEGATIVE)
    return -TAU_F * EPS_F * log_total(scores, (1, 3))


def fine_parts(distance, src_mass, src_pot, usable):
    scores = src_mass[:, None, :, None] + (src_pot[:, None, :, None] - distance) / EPS_F
    highest = jnp.max(scores, axis=2)
    summed = jnp.sum(jnp.exp(scores - highest[:, :, None, :]), axis=2)
    highest = jnp.where(usable[:, :, None], highest, NEGATIVE)
    summed = jnp.where(usable[:, :, None], summed, 0.0)
    return (highest, summed)


def local(source_coords, target_coords, source_logmass, target_logmass, pair_targets, pair_counts):
    clusters = source_coords.shape[1]
    points = source_coords.shape[2]
    listed_slots = pair_targets.shape[1]
    row_count = lax.axis_size("rows")
    col_count = lax.axis_size("cols")
    own_index = lax.axis_index("rows") * col_count + lax.axis_index("cols")
    src_cent = jnp.mean(source_coords, axis=2)
    tgt_cent = jnp.mean(target_coords, axis=2)
    src_mass = log_total(source_logmass, 1)
    tgt_mass = log_total(target_logmass, 1)
    every_tgt = lax.all_gather(
        jnp.concatenate([tgt_cent, tgt_mass[None, :]], 0), ("rows", "cols"), axis=1, tiled=True
    )
    tgt_all = jnp.zeros((every_tgt.shape[1],), jnp.float32)
    for sweep in range(C_ITERS):
        src_own = coarse_blocks(tgt_all, every_tgt[3], src_cent, every_tgt[:3])
        highest, summed = column_partials(src_mass, src_own, src_cent, every_tgt[:3])
        highest, summed = joined((highest, summed), ("rows", "cols"), merge_parts)
        tgt_all = -TAU_C * EPS_C * (highest + jnp.log(summed))
    tgt_own = lax.dynamic_slice_in_dim(tgt_all, own_index * clusters, clusters)
    remote = listed_slots - 1
    capacity = 2 * -(-(clusters * remote) // (2 * (row_count - 1)))
    slot_total = row_count * capacity
    remote_ids = pair_targets[:, 1:]
    owner_row = remote_ids // clusters // col_count
    local_ids = remote_ids % clusters
    remote_used = jnp.arange(1, listed_slots)[None, :] < pair_counts[:, None]
    flat_rows = owner_row.reshape(-1)
    flat_used = remote_used.reshape(-1)
    onehot = ((flat_rows[:, None] == jnp.arange(row_count)[None, :]) & flat_used[:, None]).astype(
        jnp.int32
    )
    before = jnp.cumsum(onehot, axis=0) - onehot
    rank_of = jnp.sum(before * onehot, axis=1)
    slot_of = jnp.where(flat_used, flat_rows * capacity + rank_of, slot_total)
    requests = (
        jnp.full((slot_total,), -1, jnp.int32).at[slot_of].set(local_ids.reshape(-1), mode="drop")
    )
    asked = lax.all_to_all(
        requests.reshape(row_count, capacity), "rows", split_axis=0, concat_axis=0, tiled=True
    )
    asked_flat = asked.reshape(-1)
    asked_index = jnp.maximum(asked_flat, 0)
    own_table = jnp.concatenate([target_coords, target_logmass[None, :, :]], 0)
    sent_cells = own_table[:, asked_index].reshape(4, row_count, capacity, points)
    got_cells = lax.all_to_all(sent_cells, "rows", split_axis=1, concat_axis=1, tiled=True)
    cell_table = jnp.concatenate([own_table, got_cells.reshape(4, slot_total, points)], 1)
    pair_index = jnp.concatenate(
        [
            jnp.arange(clusters)[:, None],
            jnp.where(remote_used, clusters + slot_of.reshape(clusters, remote), 0),
        ],
        1,
    )
    pair_cells = cell_table[:, pair_index].transpose(1, 0, 2, 3)
    usable = jnp.arange(listed_slots)[None, :] < pair_counts[:, None]
    matches = jnp.arange(clusters)[:, None] == asked_flat[None, :]
    match_table = matches.astype(jnp.float32)
    group_size = math.gcd(clusters, 4)
    group_count = clusters // group_size

    def in_groups(array):
        return array.reshape((group_count, group_size) + array.shape[1:])

    src_sorted = source_coords.transpose(1, 0, 2)
    pair_mass = pair_cells[:, 3]
    fcost = lax.map(
        lambda inputs: pair_cost(inputs[0], inputs[1][:, :3]),
        (in_groups(src_sorted), in_groups(pair_cells)),
    )
    tgt_now = jnp.broadcast_to(tgt_own[:, None], (clusters, points))
    src_now = jnp.zeros((clusters, points), jnp.float32)
    for sweep in range(F_ITERS):
        sent_pot = tgt_now[asked_index].reshape(row_count, capacity, points)
        got_pot = lax.all_to_all(sent_pot, "rows", split_axis=0, concat_axis=0, tiled=True)
        pot_table = jnp.concatenate([tgt_now, got_pot.reshape(slot_total, points)], 0)
        pair_pot = pot_table[pair_index]

        def rows_of(inputs):
            cost_group, mass_group, pot_group, usable_now = inputs
            return fine_rows(cost_group, mass_group, pot_group, usable_now)

        src_now = lax.map(
            rows_of, (fcost, in_groups(pair_mass), in_groups(pair_pot), in_groups(usable))
        ).reshape(clusters, points)

        def parts_of(inputs):
            cost_group, mass_group, pot_group, usable_now = inputs
            return fine_parts(cost_group, mass_group, pot_group, usable_now)

        highs, sums = lax.map(
            parts_of, (fcost, in_groups(source_logmass), in_groups(src_now), in_groups(usable))
        )
        highs = highs.reshape(clusters, listed_slots, points)
        sums = sums.reshape(clusters, listed_slots, points)
        back_high = (
            jnp.full((slot_total, points), NEGATIVE, jnp.float32)
            .at[slot_of]
            .set(highs[:, 1:].reshape(-1, points), mode="drop")
        )
        back_sum = (
            jnp.zeros((slot_total, points), jnp.float32)
            .at[slot_of]
            .set(sums[:, 1:].reshape(-1, points), mode="drop")
        )
        got_high, got_sum = (
            lax.all_to_all(
                back_high.reshape(row_count, capacity, points),
                "rows",
                split_axis=0,
                concat_axis=0,
                tiled=True,
            ),
            lax.all_to_all(
                back_sum.reshape(row_count, capacity, points),
                "rows",
                split_axis=0,
                concat_axis=0,
                tiled=True,
            ),
        )
        got_high = got_high.reshape(slot_total, points)
        got_sum = got_sum.reshape(slot_total, points)
        best = jnp.maximum(
            highs[:, 0],
            jnp.max(jnp.where(matches[:, :, None], got_high[None, :, :], NEGATIVE), axis=1),
        )
        scaled = got_sum * jnp.exp(got_high - best[asked_index])
        combined = sums[:, 0] * jnp.exp(highs[:, 0] - best) + jnp.dot(
            match_table, scaled, precision=lax.Precision.HIGHEST
        )
        tgt_now = -TAU_F * EPS_F * (best + jnp.log(combined))
    return (src_now, tgt_now)


def solution(mesh):
    return jax.shard_map(
        local,
        mesh=mesh,
        in_specs=(
            P(None, ("rows", "cols"), None),
            P(None, ("rows", "cols"), None),
            P(("rows", "cols"), None),
            P(("rows", "cols"), None),
            P(("rows", "cols"), None),
            P(("rows", "cols")),
        ),
        out_specs=(P(("rows", "cols"), None), P(("rows", "cols"), None)),
        check_vma=False,
    )
```

profile of v0, /device:TPU:0, one launch (start us, length us, event | category | flops | bytes accessed | tf_op | source)
XLA Modules:
  0.0 449.3 jit_solution(6709271842191339367)
XLA Ops:
  5.1 7.3 %all-to-all-start = ((s32[8,1,4]{2,1,0:T(1,128)}), s32[8,1,4]{2,1,0:T(1,128)S(1)}, u32[]{:S(2)}, u32[]{:S(2)}) async-start(s32[8,1,4]{2,1,0:T(1,128)} %bitcast.11), calls=%async_computation | async-start | bytes 8192 | tf_op jit(solution)/shard_map/all_to_all | solution.py:147
  13.5 42.1 %all-gather = f32[32,4,4]{2,1,0:T(4,128)S(1)} all-gather(f32[1,4,4]{2,1,0:T(4,128)S(1)} %bitcast.315), channel_id=1, replica_groups=mesh['rows'=8,'cols'=4] {'rows','cols'}, dimensions={0}, use_global_device_ids=true | all-gather | bytes 2112 | tf_op jit(solution)/shard_map/all_gather | solution.py:119
  56.3 36.7 %all-gather.2 = f32[32,1,128]{2,1,0:T(1,128)S(1)} all-gather(f32[1,1,128]{2,1,0:T(1,128)S(1)} %get-tuple-element.865), channel_id=1, replica_groups=mesh['rows'=8,'cols'=4] {'rows','cols'}, dimensions={0}, use_global_device_ids=true | all-gather | bytes 16896 | tf_op jit(solution)/shard_map/all_gather | solution.py:18
  93.0 38.0 %all-gather.1 = f32[32,1,128]{2,1,0:T(1,128)S(1)} all-gather(f32[1,1,128]{2,1,0:T(1,128)S(1)} %get-tuple-element.866), channel_id=1, replica_groups=mesh['rows'=8,'cols'=4] {'rows','cols'}, dimensions={0}, use_global_device_ids=true | all-gather | bytes 16896 | tf_op jit(solution)/shard_map/all_gather | solution.py:18
  132.9 36.7 %all-gather.4 = f32[32,1,128]{2,1,0:T(1,128)S(1)} all-gather(f32[1,1,128]{2,1,0:T(1,128)S(1)} %get-tuple-element.863), channel_id=1, replica_groups=mesh['rows'=8,'cols'=4] {'rows','cols'}, dimensions={0}, use_global_device_ids=true | all-gather | bytes 16896 | tf_op jit(solution)/shard_map/all_gather | solution.py:18
  169.6 38.0 %all-gather.3 = f32[32,1,128]{2,1,0:T(1,128)S(1)} all-gather(f32[1,1,128]{2,1,0:T(1,128)S(1)} %get-tuple-element.864), channel_id=1, replica_groups=mesh['rows'=8,'cols'=4] {'rows','cols'}, dimensions={0}, use_global_device_ids=true | all-gather | bytes 16896 | tf_op jit(solution)/shard_map/all_gather | solution.py:18
  209.5 36.7 %all-gather.6 = f32[32,1,128]{2,1,0:T(1,128)S(1)} all-gather(f32[1,1,128]{2,1,0:T(1,128)S(1)} %get-tuple-element.861), channel_id=1, replica_groups=mesh['rows'=8,'cols'=4] {'rows','cols'}, dimensions={0}, use_global_device_ids=true | all-gather | bytes 16896 | tf_op jit(solution)/shard_map/all_gather | solution.py:18
  246.2 38.0 %all-gather.5 = f32[32,1,128]{2,1,0:T(1,128)S(1)} all-gather(f32[1,1,128]{2,1,0:T(1,128)S(1)} %get-tuple-element.862), channel_id=1, replica_groups=mesh['rows'=8,'cols'=4] {'rows','cols'}, dimensions={0}, use_global_device_ids=true | all-gather | bytes 16896 | tf_op jit(solution)/shard_map/all_gather | solution.py:18
  286.1 36.7 %all-gather.8 = f32[32,1,128]{2,1,0:T(1,128)S(1)} all-gather(f32[1,1,128]{2,1,0:T(1,128)S(1)} %get-tuple-element.859), channel_id=1, replica_groups=mesh['rows'=8,'cols'=4] {'rows','cols'}, dimensions={0}, use_global_device_ids=true | all-gather | bytes 16896 | tf_op jit(solution)/shard_map/all_gather | solution.py:18
  322.7 38.0 %all-gather.7 = f32[32,1,128]{2,1,0:T(1,128)S(1)} all-gather(f32[1,1,128]{2,1,0:T(1,128)S(1)} %get-tuple-element.860), channel_id=1, replica_groups=mesh['rows'=8,'cols'=4] {'rows','cols'}, dimensions={0}, use_global_device_ids=true | all-gather | bytes 16896 | tf_op jit(solution)/shard_map/all_gather | solution.py:18
  364.7 3.3 all-to-all-start.2
  369.4 5.1 %all-to-all-done.2 = f32[8,4,128]{2,1,0:T(4,128)S(1)} async-done(((f32[8,4,128]{2,1,0:T(4,128)}), f32[8,4,128]{2,1,0:T(4,128)S(1)}, u32[]{:S(2)}, u32[]{:S(2)}) %all-to-all-start.2) | async-done | bytes 16416 | tf_op jit(solution)/shard_map/all_to_all | solution.py:183
  374.6 3.3 all-to-all-start.1
  378.7 6.1 %all-to-all-done.1 = f32[4,8,4,128]{3,0,2,1:T(4,128)S(1)} async-done(((f32[4,8,4,128]{3,0,2,1:T(4,128)}), f32[4,8,4,128]{3,0,2,1:T(4,128)S(1)}, u32[]{:S(2)}, u32[]{:S(2)}) %all-to-all-start.1) | async-done | bytes 65568 | tf_op jit(solution)/shard_map/all_to_all | solution.py:154
  392.2 3.3 all-to-all-start.3
  396.8 5.3 %all-to-all-done.3 = f32[8,4,128]{2,1,0:T(4,128)S(1)} async-done(((f32[8,4,128]{2,1,0:T(4,128)}), f32[8,4,128]{2,1,0:T(4,128)S(1)}, u32[]{:S(2)}, u32[]{:S(2)}) %all-to-all-start.3) | async-done | bytes 16416 | tf_op jit(solution)/shard_map/all_to_all | solution.py:215
  402.1 3.3 all-to-all-start.4
  406.1 5.8 %all-to-all-done.4 = f32[8,4,128]{2,1,0:T(4,128)S(1)} async-done(((f32[8,4,128]{2,1,0:T(4,128)}), f32[8,4,128]{2,1,0:T(4,128)S(1)}, u32[]{:S(2)}, u32[]{:S(2)}) %all-to-all-start.4) | async-done | bytes 16416 | tf_op jit(solution)/shard_map/all_to_all | solution.py:222
  412.6 8.9 %all_to_all.44 = f32[8,4,128]{2,1,0:T(4,128)S(1)} all-to-all(f32[8,4,128]{2,1,0:T(4,128)S(1)} %bitcast.297), channel_id=1, replica_groups=mesh['rows'=8,'cols'=4] {'rows'}, dimensions={0} | all-to-all | bytes 32768 | tf_op jit(solution)/shard_map/all_to_all | solution.py:183
  423.4 1.6 exponential_reduce_fusion.1
  428.9 3.3 all-to-all-start.6
  433.5 5.3 %all-to-all-done.6 = f32[8,4,128]{2,1,0:T(4,128)S(1)} async-done(((f32[8,4,128]{2,1,0:T(4,128)}), f32[8,4,128]{2,1,0:T(4,128)S(1)}, u32[]{:S(2)}, u32[]{:S(2)}) %all-to-all-start.6) | async-done | bytes 16416 | tf_op jit(solution)/shard_map/all_to_all | solution.py:215
  438.8 3.3 all-to-all-start.7
  442.8 5.8 %all-to-all-done.7 = f32[8,4,128]{2,1,0:T(4,128)S(1)} async-done(((f32[8,4,128]{2,1,0:T(4,128)}), f32[8,4,128]{2,1,0:T(4,128)S(1)}, u32[]{:S(2)}, u32[]{:S(2)}) %all-to-all-start.7) | async-done | bytes 16416 | tf_op jit(solution)/shard_map/all_to_all | solution.py:222
  (270 shorter events, 39.6 us)
Async XLA Ops:
  0.6 11.8 %copy-start.5 = (s32[4]{0:T(128)S(1)}, s32[4]{0:T(128)}, u32[]{:S(2)}) copy-start(s32[4]{0:T(128)} %param.19) | copy-start | bytes 52
  1.5 11.0 %copy-start = (f32[4,128]{1,0:T(4,128)S(1)}, f32[4,128]{1,0:T(4,128)}, u32[]{:S(2)}) copy-start(f32[4,128]{1,0:T(4,128)} %param.17) | copy-start | bytes 6148
  1.6 11.0 %copy-start.1 = (f32[4,128]{1,0:T(4,128)S(1)}, f32[4,128]{1,0:T(4,128)}, u32[]{:S(2)}) copy-start(f32[4,128]{1,0:T(4,128)} %param.16) | copy-start | bytes 6148
  2.5 10.6 %copy-start.2 = (f32[3,4,128]{2,1,0:T(4,128)S(1)}, f32[3,4,128]{2,1,0:T(4,128)}, u32[]{:S(2)}) copy-start(f32[3,4,128]{2,1,0:T(4,128)} %param.15) | copy-start | bytes 18436
  3.5 9.7 %copy-start.3 = (f32[3,4,128]{2,1,0:T(4,128)S(1)}, f32[3,4,128]{2,1,0:T(4,128)}, u32[]{:S(2)}) copy-start(f32[3,4,128]{2,1,0:T(4,128)} %param.14) | copy-start | bytes 18436
  5.1 357.1 %all-to-all-start = ((s32[8,1,4]{2,1,0:T(1,128)}), s32[8,1,4]{2,1,0:T(1,128)S(1)}, u32[]{:S(2)}, u32[]{:S(2)}) async-start(s32[8,1,4]{2,1,0:T(1,128)} %bitcast.11), calls=%async_computation | async-start | bytes 8192 | tf_op jit(solution)/shard_map/all_to_all | solution.py:147
  364.7 9.8 %all-to-all-start.2 = ((f32[8,4,128]{2,1,0:T(4,128)}), f32[8,4,128]{2,1,0:T(4,128)S(1)}, u32[]{:S(2)}, u32[]{:S(2)}) async-start(f32[8,4,128]{2,1,0:T(4,128)} %bitcast.63), calls=%async_computation.2 | async-start | bytes 32768 | tf_op jit(solution)/shard_map/all_to_all | solution.py:183
  374.6 10.2 %all-to-all-start.1 = ((f32[4,8,4,128]{3,0,2,1:T(4,128)}), f32[4,8,4,128]{3,0,2,1:T(4,128)S(1)}, u32[]{:S(2)}, u32[]{:S(2)}) async-start(f32[4,8,4,128]{3,0,2,1:T(4,128)} %bitcast.13), calls=%async_computation.1 | async-start | bytes 131072 | tf_op jit(solution)/shard_map/all_to_all | solution.py:154
  392.2 9.9 %all-to-all-start.3 = ((f32[8,4,128]{2,1,0:T(4,128)}), f32[8,4,128]{2,1,0:T(4,128)S(1)}, u32[]{:S(2)}, u32[]{:S(2)}) async-start(f32[8,4,128]{2,1,0:T(4,128)} %bitcast.75), calls=%async_computation.3 | async-start | bytes 32768 | tf_op jit(solution)/shard_map/all_to_all | solution.py:215
  402.1 9.8 %all-to-all-start.4 = ((f32[8,4,128]{2,1,0:T(4,128)}), f32[8,4,128]{2,1,0:T(4,128)S(1)}, u32[]{:S(2)}, u32[]{:S(2)}) async-start(f32[8,4,128]{2,1,0:T(4,128)} %bitcast.78), calls=%async_computation.4 | async-start | bytes 32768 | tf_op jit(solution)/shard_map/all_to_all | solution.py:222
  425.1 2.5 copy-start.4
  428.9 9.9 %all-to-all-start.6 = ((f32[8,4,128]{2,1,0:T(4,128)}), f32[8,4,128]{2,1,0:T(4,128)S(1)}, u32[]{:S(2)}, u32[]{:S(2)}) async-start(f32[8,4,128]{2,1,0:T(4,128)} %bitcast.84), calls=%async_computation.6 | async-start | bytes 32768 | tf_op jit(solution)/shard_map/all_to_all | solution.py:215
  438.8 9.8 %all-to-all-start.7 = ((f32[8,4,128]{2,1,0:T(4,128)}), f32[8,4,128]{2,1,0:T(4,128)S(1)}, u32[]{:S(2)}, u32[]{:S(2)}) async-start(f32[8,4,128]{2,1,0:T(4,128)} %bitcast.87), calls=%async_computation.7 | async-start | bytes 32768 | tf_op jit(solution)/shard_map/all_to_all | solution.py:222
where the time goes:
time: 450 us; the launch traced here: 449 us
  blocking collectives  350 us (78%)
  waiting for transfers between devices  33.4 us (7%)
  starting transfers between devices  27.3 us (6%)
  other arithmetic  21 us (5%)
  local copies, waits for them, and re-layouts  13.9 us (3%)
    all_gather x8, blocking collectives, joined(): gathered = jax.tree.map(lambda a: lax.all_gather(a, axis), part)  299 us
    all_gather x1, blocking collectives, local(): lax.all_gather(jnp.concatenate([tgt_cent, tgt_mass[None, :]], 0), ('rows'...  42.1 us
    all_to_all x2, waiting for transfers between devices, local(): lax.all_to_all(back_sum.reshape(row_count, capacity, points), 'rows', spl...  11.7 us
    all_to_all x2, waiting for transfers between devices, local(): lax.all_to_all(back_high.reshape(row_count, capacity, points), 'rows', sp...  10.5 us
  transfers between devices with their start and end apart: 7, of which 6 were waited for; matrix products, arithmetic and copies ran while one was open for 3% of the time, Pallas kernels for 0%

commit v1 on v0

--- a/solution.py
+++ b/solution.py
@@ -116,9 +116,23 @@
     tgt_cent = jnp.mean(target_coords, axis=2)
     src_mass = log_total(source_logmass, 1)
     tgt_mass = log_total(target_logmass, 1)
-    every_tgt = lax.all_gather(
-        jnp.concatenate([tgt_cent, tgt_mass[None, :]], 0), ("rows", "cols"), axis=1, tiled=True
-    )
+    value = jnp.concatenate([tgt_cent, tgt_mass[None, :]], 0)
+    ways, here, k = (
+        lax.axis_size(("rows", "cols")),
+        lax.axis_index(("rows", "cols")),
+        value.shape[1],
+    )
+    line, have = (value, 1)
+    while have < ways:
+        line = jnp.concatenate(
+            [
+                line,
+                lax.ppermute(line, ("rows", "cols"), [(d, (d - have) % ways) for d in range(ways)]),
+            ],
+            axis=1,
+        )
+        have = 2 * have
+    every_tgt = jnp.roll(line, here * k, axis=1)
     tgt_all = jnp.zeros((every_tgt.shape[1],), jnp.float32)
     for sweep in range(C_ITERS):
         src_own = coarse_blocks(tgt_all, every_tgt[3], src_cent, every_tgt[:3])

time: 450 us -> 435 us (0.967)
  blocking collectives: 350 us -> 315 us
  waiting for transfers between devices: 33.4 us -> 45.7 us
  starting transfers between devices: 27.3 us -> 34.1 us
    all_gather x1 -> x0, blocking collectives: 42.1 us -> none  [local(): lax.all_gather(jnp.concatenate([tgt_cent, tgt_mass[None, :]], 0), ('rows'...]
    ppermute x0 -> x5, waiting for transfers between devices: none -> 12.4 us  [local(): lax.ppermute(line, ('rows', 'cols'), [(d, (d - have) % ways) for d in ran...]
    all_gather x8, blocking collectives: 299 us -> 306 us  [joined(): gathered = jax.tree.map(lambda a: lax.all_gather(a, axis), part)]
    ppermute x0 -> x5, starting transfers between devices: none -> 6.86 us  [local(): lax.ppermute(line, ('rows', 'cols'), [(d, (d - have) % ways) for d in ran...]
  transfers between devices with their start and end apart: 7 -> 12, of which waited for: 6 -> 11; matrix products, arithmetic and copies ran while one was open for 3% -> 2% of each run, Pallas kernels for 0% -> 0%
where the time goes in v1:
time: 435 us; the launch traced here: 434 us
  blocking collectives  315 us (72%)
  waiting for transfers between devices  45.7 us (11%)
  starting transfers between devices  34.1 us (8%)
  other arithmetic  21.2 us (5%)
  local copies, waits for them, and re-layouts  14 us (3%)
    all_gather x8, blocking collectives, joined(): gathered = jax.tree.map(lambda a: lax.all_gather(a, axis), part)  306 us
    ppermute x5, waiting for transfers between devices, local(): lax.ppermute(line, ('rows', 'cols'), [(d, (d - have) % ways) for d in ran...  12.4 us
    all_to_all x2, waiting for transfers between devices, local(): lax.all_to_all(back_sum.reshape(row_count, capacity, points), 'rows', spl...  11.7 us
    all_to_all x2, waiting for transfers between devices, local(): lax.all_to_all(back_high.reshape(row_count, capacity, points), 'rows', sp...  10.5 us
    all_to_all x1, blocking collectives, local(): lax.all_to_all(sent_pot, 'rows', split_axis=0, concat_axis=0, tiled=True)  8.94 us
  transfers between devices with their start and end apart: 12, of which 11 were waited for; matrix products, arithmetic and copies ran while one was open for 2% of the time, Pallas kernels for 0%

profile of v1, /device:TPU:0, one launch (start us, length us, event | category | flops | bytes accessed | tf_op | source)
XLA Modules:
  0.0 434.3 jit_solution(1252190427946943397)
XLA Ops:
  5.0 7.3 %all-to-all-start = ((s32[8,1,4]{2,1,0:T(1,128)}), s32[8,1,4]{2,1,0:T(1,128)S(1)}, u32[]{:S(2)}, u32[]{:S(2)}) async-start(s32[8,1,4]{2,1,0:T(1,128)} %bitcast.11), calls=%async_computation | async-start | bytes 8192 | tf_op jit(solution)/shard_map/all_to_all | solution.py:161
  12.7 4.6 %collective-permute-start = (f32[4,4]{1,0:T(4,128)S(1)}, f32[4,4]{1,0:T(4,128)S(1)}, u32[]{:S(2)}, u32[]{:S(2)}) collective-permute-start(f32[4,4]{1,0:T(4,128)S(1)} %pad_maximum_fusion.4), channel_id=1, source_target_pairs={{0,31},{1,0},{2,1},{3,2},{4,3},{5,4},{6,5},{7,6},{8,7},{9,8},{10,9... | collective-permute-start | bytes 200 | tf_op jit(solution)/shard_map/ppermute | solution.py:130
  29.8 4.5 %collective-permute-done.4 = f32[4,64]{1,0:T(4,128)S(1)} collective-permute-done((f32[4,64]{1,0:T(4,128)S(1)}, f32[4,64]{1,0:T(4,128)S(1)}, u32[]{:S(2)}, u32[]{:S(2)}) %collective-permute-start.4) | collective-permute-done | bytes 1056 | tf_op jit(solution)/shard_map/ppermute | solution.py:130
  35.0 45.6 %all-gather = f32[32,1,128]{2,1,0:T(1,128)S(1)} all-gather(f32[1,1,128]{2,1,0:T(1,128)S(1)} %get-tuple-element.866), channel_id=1, replica_groups=mesh['rows'=8,'cols'=4] {'rows','cols'}, dimensions={0}, use_global_device_ids=true | all-gather | bytes 16896 | tf_op jit(solution)/shard_map/all_gather | solution.py:18
  80.6 36.7 %all-gather.1 = f32[32,1,128]{2,1,0:T(1,128)S(1)} all-gather(f32[1,1,128]{2,1,0:T(1,128)S(1)} %get-tuple-element.865), channel_id=1, replica_groups=mesh['rows'=8,'cols'=4] {'rows','cols'}, dimensions={0}, use_global_device_ids=true | all-gather | bytes 16896 | tf_op jit(solution)/shard_map/all_gather | solution.py:18
  119.1 38.0 %all-gather.2 = f32[32,1,128]{2,1,0:T(1,128)S(1)} all-gather(f32[1,1,128]{2,1,0:T(1,128)S(1)} %get-tuple-element.864), channel_id=1, replica_groups=mesh['rows'=8,'cols'=4] {'rows','cols'}, dimensions={0}, use_global_device_ids=true | all-gather | bytes 16896 | tf_op jit(solution)/shard_map/all_gather | solution.py:18
  157.2 36.7 %all-gather.3 = f32[32,1,128]{2,1,0:T(1,128)S(1)} all-gather(f32[1,1,128]{2,1,0:T(1,128)S(1)} %get-tuple-element.863), channel_id=1, replica_groups=mesh['rows'=8,'cols'=4] {'rows','cols'}, dimensions={0}, use_global_device_ids=true | all-gather | bytes 16896 | tf_op jit(solution)/shard_map/all_gather | solution.py:18
  195.7 38.0 %all-gather.4 = f32[32,1,128]{2,1,0:T(1,128)S(1)} all-gather(f32[1,1,128]{2,1,0:T(1,128)S(1)} %get-tuple-element.862), channel_id=1, replica_groups=mesh['rows'=8,'cols'=4] {'rows','cols'}, dimensions={0}, use_global_device_ids=true | all-gather | bytes 16896 | tf_op jit(solution)/shard_map/all_gather | solution.py:18
  233.8 36.7 %all-gather.5 = f32[32,1,128]{2,1,0:T(1,128)S(1)} all-gather(f32[1,1,128]{2,1,0:T(1,128)S(1)} %get-tuple-element.861), channel_id=1, replica_groups=mesh['rows'=8,'cols'=4] {'rows','cols'}, dimensions={0}, use_global_device_ids=true | all-gather | bytes 16896 | tf_op jit(solution)/shard_map/all_gather | solution.py:18
  272.3 38.0 %all-gather.6 = f32[32,1,128]{2,1,0:T(1,128)S(1)} all-gather(f32[1,1,128]{2,1,0:T(1,128)S(1)} %get-tuple-element.860), channel_id=1, replica_groups=mesh['rows'=8,'cols'=4] {'rows','cols'}, dimensions={0}, use_global_device_ids=true | all-gather | bytes 16896 | tf_op jit(solution)/shard_map/all_gather | solution.py:18
  310.4 36.7 %all-gather.7 = f32[32,1,128]{2,1,0:T(1,128)S(1)} all-gather(f32[1,1,128]{2,1,0:T(1,128)S(1)} %get-tuple-element.859), channel_id=1, replica_groups=mesh['rows'=8,'cols'=4] {'rows','cols'}, dimensions={0}, use_global_device_ids=true | all-gather | bytes 16896 | tf_op jit(solution)/shard_map/all_gather | solution.py:18
  349.7 3.3 all-to-all-start.2
  354.4 5.1 %all-to-all-done.2 = f32[8,4,128]{2,1,0:T(4,128)S(1)} async-done(((f32[8,4,128]{2,1,0:T(4,128)}), f32[8,4,128]{2,1,0:T(4,128)S(1)}, u32[]{:S(2)}, u32[]{:S(2)}) %all-to-all-start.2) | async-done | bytes 16416 | tf_op jit(solution)/shard_map/all_to_all | solution.py:197
  359.5 3.3 all-to-all-start.1
  363.7 6.1 %all-to-all-done.1 = f32[4,8,4,128]{3,0,2,1:T(4,128)S(1)} async-done(((f32[4,8,4,128]{3,0,2,1:T(4,128)}), f32[4,8,4,128]{3,0,2,1:T(4,128)S(1)}, u32[]{:S(2)}, u32[]{:S(2)}) %all-to-all-start.1) | async-done | bytes 65568 | tf_op jit(solution)/shard_map/all_to_all | solution.py:168
  377.2 3.3 all-to-all-start.3
  381.8 5.3 %all-to-all-done.3 = f32[8,4,128]{2,1,0:T(4,128)S(1)} async-done(((f32[8,4,128]{2,1,0:T(4,128)}), f32[8,4,128]{2,1,0:T(4,128)S(1)}, u32[]{:S(2)}, u32[]{:S(2)}) %all-to-all-start.3) | async-done | bytes 16416 | tf_op jit(solution)/shard_map/all_to_all | solution.py:229
  387.0 3.3 all-to-all-start.4
  391.1 5.8 %all-to-all-done.4 = f32[8,4,128]{2,1,0:T(4,128)S(1)} async-done(((f32[8,4,128]{2,1,0:T(4,128)}), f32[8,4,128]{2,1,0:T(4,128)S(1)}, u32[]{:S(2)}, u32[]{:S(2)}) %all-to-all-start.4) | async-done | bytes 16416 | tf_op jit(solution)/shard_map/all_to_all | solution.py:236
  397.6 8.9 %all_to_all.44 = f32[8,4,128]{2,1,0:T(4,128)S(1)} all-to-all(f32[8,4,128]{2,1,0:T(4,128)S(1)} %bitcast.286), channel_id=1, replica_groups=mesh['rows'=8,'cols'=4] {'rows'}, dimensions={0} | all-to-all | bytes 32768 | tf_op jit(solution)/shard_map/all_to_all | solution.py:197
  413.9 3.3 all-to-all-start.6
  418.5 5.3 %all-to-all-done.6 = f32[8,4,128]{2,1,0:T(4,128)S(1)} async-done(((f32[8,4,128]{2,1,0:T(4,128)}), f32[8,4,128]{2,1,0:T(4,128)S(1)}, u32[]{:S(2)}, u32[]{:S(2)}) %all-to-all-start.6) | async-done | bytes 16416 | tf_op jit(solution)/shard_map/all_to_all | solution.py:229
  423.8 3.3 all-to-all-start.7
  427.8 5.8 %all-to-all-done.7 = f32[8,4,128]{2,1,0:T(4,128)S(1)} async-done(((f32[8,4,128]{2,1,0:T(4,128)}), f32[8,4,128]{2,1,0:T(4,128)S(1)}, u32[]{:S(2)}, u32[]{:S(2)}) %all-to-all-start.7) | async-done | bytes 16416 | tf_op jit(solution)/shard_map/all_to_all | solution.py:236
  (284 shorter events, 51.7 us)
Async XLA Ops:
  0.6 11.7 %copy-start = (f32[4,128]{1,0:T(4,128)S(1)}, f32[4,128]{1,0:T(4,128)}, u32[]{:S(2)}) copy-start(f32[4,128]{1,0:T(4,128)} %param.17) | copy-start | bytes 6148
  0.6 12.0 %copy-start.2 = (f32[3,4,128]{2,1,0:T(4,128)S(1)}, f32[3,4,128]{2,1,0:T(4,128)}, u32[]{:S(2)}) copy-start(f32[3,4,128]{2,1,0:T(4,128)} %param.15) | copy-start | bytes 18436
  3.3 14.1 %copy-start.5 = (s32[4]{0:T(128)S(1)}, s32[4]{0:T(128)}, u32[]{:S(2)}) copy-start(s32[4]{0:T(128)} %param.19) | copy-start | bytes 52
  3.4 14.1 %copy-start.3 = (f32[3,4,128]{2,1,0:T(4,128)S(1)}, f32[3,4,128]{2,1,0:T(4,128)}, u32[]{:S(2)}) copy-start(f32[3,4,128]{2,1,0:T(4,128)} %param.14) | copy-start | bytes 18436
  3.6 14.0 %copy-start.1 = (f32[4,128]{1,0:T(4,128)S(1)}, f32[4,128]{1,0:T(4,128)}, u32[]{:S(2)}) copy-start(f32[4,128]{1,0:T(4,128)} %param.16) | copy-start | bytes 6148
  5.0 21.6 %all-to-all-start = ((s32[8,1,4]{2,1,0:T(1,128)}), s32[8,1,4]{2,1,0:T(1,128)S(1)}, u32[]{:S(2)}, u32[]{:S(2)}) async-start(s32[8,1,4]{2,1,0:T(1,128)} %bitcast.11), calls=%async_computation | async-start | bytes 8192 | tf_op jit(solution)/shard_map/all_to_all | solution.py:161
  12.7 5.9 %collective-permute-start = (f32[4,4]{1,0:T(4,128)S(1)}, f32[4,4]{1,0:T(4,128)S(1)}, u32[]{:S(2)}, u32[]{:S(2)}) collective-permute-start(f32[4,4]{1,0:T(4,128)S(1)} %pad_maximum_fusion.4), channel_id=1, source_target_pairs={{0,31},{1,0},{2,1},{3,2},{4,3},{5,4},{6,5},{7,6},{8,7},{9,8},{10,9... | collective-permute-start | bytes 200 | tf_op jit(solution)/shard_map/ppermute | solution.py:130
  18.7 3.6 collective-permute-start.1
  22.4 3.6 collective-permute-start.2
  26.1 3.6 collective-permute-start.3
  29.7 4.5 %collective-permute-start.4 = (f32[4,64]{1,0:T(4,128)S(1)}, f32[4,64]{1,0:T(4,128)S(1)}, u32[]{:S(2)}, u32[]{:S(2)}) collective-permute-start(f32[4,64]{1,0:T(4,128)S(1)} %concatenate.69), channel_id=1, source_target_pairs={{0,16},{1,17},{2,18},{3,19},{4,20},{5,21},{6,22},{7,23},{8,24},{9,... | collective-permute-start | bytes 3080 | tf_op jit(solution)/shard_map/ppermute | solution.py:130
  349.7 9.8 %all-to-all-start.2 = ((f32[8,4,128]{2,1,0:T(4,128)}), f32[8,4,128]{2,1,0:T(4,128)S(1)}, u32[]{:S(2)}, u32[]{:S(2)}) async-start(f32[8,4,128]{2,1,0:T(4,128)} %bitcast.59), calls=%async_computation.2 | async-start | bytes 32768 | tf_op jit(solution)/shard_map/all_to_all | solution.py:197
  359.5 10.2 %all-to-all-start.1 = ((f32[4,8,4,128]{3,0,2,1:T(4,128)}), f32[4,8,4,128]{3,0,2,1:T(4,128)S(1)}, u32[]{:S(2)}, u32[]{:S(2)}) async-start(f32[4,8,4,128]{3,0,2,1:T(4,128)} %bitcast.13), calls=%async_computation.1 | async-start | bytes 131072 | tf_op jit(solution)/shard_map/all_to_all | solution.py:168
  377.2 9.9 %all-to-all-start.3 = ((f32[8,4,128]{2,1,0:T(4,128)}), f32[8,4,128]{2,1,0:T(4,128)S(1)}, u32[]{:S(2)}, u32[]{:S(2)}) async-start(f32[8,4,128]{2,1,0:T(4,128)} %bitcast.71), calls=%async_computation.3 | async-start | bytes 32768 | tf_op jit(solution)/shard_map/all_to_all | solution.py:229
  387.0 9.8 %all-to-all-start.4 = ((f32[8,4,128]{2,1,0:T(4,128)}), f32[8,4,128]{2,1,0:T(4,128)S(1)}, u32[]{:S(2)}, u32[]{:S(2)}) async-start(f32[8,4,128]{2,1,0:T(4,128)} %bitcast.74), calls=%async_computation.4 | async-start | bytes 32768 | tf_op jit(solution)/shard_map/all_to_all | solution.py:236
  410.0 2.5 copy-start.4
  413.9 9.9 %all-to-all-start.6 = ((f32[8,4,128]{2,1,0:T(4,128)}), f32[8,4,128]{2,1,0:T(4,128)S(1)}, u32[]{:S(2)}, u32[]{:S(2)}) async-start(f32[8,4,128]{2,1,0:T(4,128)} %bitcast.80), calls=%async_computation.6 | async-start | bytes 32768 | tf_op jit(solution)/shard_map/all_to_all | solution.py:229
  423.8 9.8 %all-to-all-start.7 = ((f32[8,4,128]{2,1,0:T(4,128)}), f32[8,4,128]{2,1,0:T(4,128)S(1)}, u32[]{:S(2)}, u32[]{:S(2)}) async-start(f32[8,4,128]{2,1,0:T(4,128)} %bitcast.83), calls=%async_computation.7 | async-start | bytes 32768 | tf_op jit(solution)/shard_map/all_to_all | solution.py:236
